TPU v7x, 32 devices: a whole 2x2x4 slice. The times are simulated.
32 devices in a mesh: grid: 8 (over y, x, core), mode: 4 (over z).
Axes of the slice: x: 2, y: 2, z: 4, core: 2. Of those that a mesh axis runs over, the one named last changes fastest.
Arguments:
- held_modes: bfloat16 [224, 3, 32, 4, 128], P('mode', None, 'grid'), may hold values from -6 to 6
- new_modes: bfloat16 [32, 3, 32, 4, 128], P('mode', None, 'grid'), may hold values from -6 to 6
Outputs:
- new_third: float32 [256, 8192], P('grid', 'mode')
- held_third_new_first: float32 [256, 7168], P('grid', 'mode')
- held_third_new_second: float32 [224, 7168], P('grid', 'mode')
All inputs are finite; a program needn't handle non-finite values.
Results may differ from a plain program's by a relative error of at most 0.0042.
Values may be sent and summed in bfloat16 or wider, within the bound.
No kernel may reach another device: no remote copies, remote signals or barrier semaphores. Data moves between devices by JAX's collectives and lax.ppermute only.
A program may use at most 128 MiB of HBM per device.

v0:
```python
import functools
import math

import jax
import jax.numpy as jnp
from jax import lax
from jax.experimental import pallas as pl
from jax.experimental.pallas import tpu as pltpu
from jax.sharding import PartitionSpec as P


F32 = jnp.float32
BF16 = jnp.bfloat16
LANES = 128
NT = (((1,), (1,)), ((), ()))


def shift(count, step):
    return [(i, (i + step) % count) for i in range(count)]


def fill_slopes(before, here, after, slopes):
    comps, _, cells = here.shape
    rows_y = cells // LANES

    def put(entry, y, difference):
        slopes[entry, y] = (difference * 0.5).astype(BF16).astype(F32)

    for a in range(comps):
        line = here[a].astype(F32)
        along_x = after[a].astype(F32) - before[a].astype(F32)
        parts = [line[:, y * LANES : (y + 1) * LANES] for y in range(rows_y)]
        for y in range(rows_y):
            put(a * 3, y, along_x[:, y * LANES : (y + 1) * LANES])
            put(a * 3 + 1, y, parts[(y + 1) % rows_y] - parts[(y - 1) % rows_y])
            put(a * 3 + 2, y, pltpu.roll(parts[y], LANES - 1, 1) - pltpu.roll(parts[y], 1, 1))


def plane_kernel(first, last, held_own, new_own, owners, blocks, me_ref, before, here, after, *rest):
    sources, rest = rest[:blocks], rest[blocks:]
    totals = None
    if not first:
        totals, rest = rest[0], rest[1:]
    outs, rest = rest[: 1 + last], rest[1 + last :]
    every, every_held, wide, slopes, fill_a, fill_b, fill_c = rest
    comps, _, cells = here.shape
    held, new = held_own * blocks, new_own * blocks
    total = held + new
    group = total // new
    steps = held_own // group
    lines = cells // LANES
    half = total // 2

    fill_slopes(before, here, after, slopes)
    for s, source in enumerate(sources):
        owner = lax.rem(me_ref[0] + blocks - s, blocks)
        low = pl.multiple_of(owner * held_own, 8)
        low_new = pl.multiple_of(held + owner * new_own, 8)
        for a in range(comps):
            block = source[a].astype(F32)
            columns = slice(a * cells, (a + 1) * cells)
            wide[pl.ds(low, held_own), columns] = block[:held_own]
            wide[pl.ds(low_new, new_own), columns] = block[held_own:]

    def by_owner(target, count):
        rows = total // owners
        for parity in range(2):
            start = pl.multiple_of(jnp.where(me_ref[1] == parity, 0, half), half)
            for low in range(0, comps * cells, LANES):
                columns = slice(low, low + LANES)
                parts = [
                    wide[g * count // owners : g * count // owners + rows, columns]
                    for g in range(parity, owners, 2)
                ]
                target[pl.ds(start, half), columns] = jnp.concatenate(parts, 0).astype(BF16)

    by_owner(every, total)
    by_owner(every_held, held)

    def slope_rows(k, y, count):
        rows = [slopes[entry, y, pl.ds(k, 8, stride=0), :] for entry in range(3 * comps)]
        return [jnp.concatenate([row] * (count // 8), 0) for row in rows]

    def at(b, y):
        return slice(b * cells + y * LANES, b * cells + (y + 1) * LANES)

    def speeds(low, count, y):
        return [wide[low : low + count, at(a, y)] for a in range(comps)]

    def along(v, g, terms):
        return (v[0] * g[terms[0]] + v[1] * g[terms[1]] + v[2] * g[terms[2]]).astype(BF16)

    def fill_held(buffer, step, entries):
        for y in range(lines):
            for kk in range(group):
                g = slope_rows(step * group + kk, y, 16)
                for part in range(0, new, 16):
                    v = speeds(held + part, 16, y)
                    low = kk * new + part
                    for c in range(3):
                        buffer[low : low + 16, at(c, y)] = along(v, g, entries(c))

    def fill_new(buffer, step, entries):
        for y in range(lines):
            g = slope_rows(held_own + step, y, 16)
            for low in range(0, total, 16):
                v = speeds(low, 16, y)
                for c in range(3):
                    buffer[low : low + 16, at(c, y)] = along(v, g, entries(c))

    def onto_first(c):
        return (c, 3 + c, 6 + c)

    def onto_second(c):
        return (3 * c, 3 * c + 1, 3 * c + 2)

    def add(tile, rows, buffer):
        value = lax.dot_general(rows[...], buffer[...], NT, preferred_element_type=F32)
        columns = pl.ds(pl.multiple_of(tile * total, LANES), total)
        value = value if first else totals[:, columns] + value
        for i, out in enumerate(outs):
            out[:, columns] = value[i * half : (i + 1) * half] if last else value

    def one(step, carry):
        @pl.when(step == 0)
        def _():
            fill_new(fill_a, step, onto_second)

        @pl.when(step > 0)
        def _():
            fill_new(fill_a, step, onto_second)
            add(new_own + steps + step - 1, every_held, fill_c)

        @pl.when(step < steps)
        def _():
            fill_held(fill_b, step, onto_first)
            add(step, every, fill_a)

        @pl.when(step < steps)
        def _():
            fill_held(fill_c, step, onto_second)
            add(new_own + step, every, fill_b)

        @pl.when(step >= steps)
        def _():
            add(step, every, fill_a)

        return carry

    lax.fori_loop(0, new_own, one, 0)


def plane_terms(place, before, here, after, sources, totals, last, held_own, new_own, owners):
    comps, own, cells = here.shape
    blocks = len(sources)
    total, new, depth = own * blocks, new_own * blocks, comps * cells
    vmem = pl.BlockSpec(memory_space=pltpu.VMEM)
    operands = [place, before, here, after, *sources]
    aliases = {}
    if totals is not None:
        aliases = {} if last else {len(operands): 0}
        operands.append(totals)
    columns = new_own * total + 2 * held_own * new
    vmem_mib = 16
    rows = [total // 2] * 2 if last else [total]
    return pl.pallas_call(
        functools.partial(plane_kernel, totals is None, last, held_own, new_own, owners, blocks),
        out_shape=[jax.ShapeDtypeStruct((n, columns), F32) for n in rows],
        in_specs=[pl.BlockSpec(memory_space=pltpu.SMEM)] + [vmem] * (len(operands) - 1),
        out_specs=[vmem] * len(rows),
        scratch_shapes=[
            pltpu.VMEM((total, depth), BF16),
            pltpu.VMEM((total, depth), BF16),
            pltpu.VMEM((total, depth), F32),
            pltpu.VMEM((3 * comps, cells // LANES, own, LANES), F32),
            pltpu.VMEM((total, depth), BF16),
            pltpu.VMEM((total, depth), BF16),
            pltpu.VMEM((total, depth), BF16),
        ],
        input_output_aliases=aliases,
        compiler_params=pltpu.CompilerParams(vmem_limit_bytes=vmem_mib * 2**20),
        name="plane_terms",
    )(*operands)


def scatter_sum(held, order):
    count = lax.axis_size("grid")
    bits = count.bit_length() - 1
    me = lax.axis_index("grid")
    left = list(range(bits - 1, 0, -1))
    for bit in order:
        axis = left.index(bit)
        left.pop(axis)
        mine = (me >> bit) & 1
        send = lax.dynamic_index_in_dim(held, 1 - mine, axis, keepdims=False).astype(BF16)
        keep = lax.dynamic_index_in_dim(held, mine, axis, keepdims=False)
        held = keep + lax.ppermute(send, "grid", [(i, i ^ (1 << bit)) for i in range(count)]).astype(F32)
    return held


def gather_planes(own, blocks):
    arrived = []
    for plane in own:
        parts = [plane]
        for s in range(1, blocks):
            straight = s == blocks - 1
            source = plane if straight else parts[-1]
            parts.append(lax.ppermute(source, "mode", shift(blocks, -1 if straight else 1)))
        arrived.append(parts)
    return arrived


def per_device(held_modes, new_modes):
    held_own, new_own = held_modes.shape[0], new_modes.shape[0]
    comps, planes = held_modes.shape[1:3]
    cells = held_modes.shape[3] * held_modes.shape[4]
    count, blocks = lax.axis_size("grid"), lax.axis_size("mode")
    bits = count.bit_length() - 1
    weighting = 1.0 / math.sqrt(planes * cells * count)
    own = jnp.concatenate([held_modes, new_modes], 0)
    own = own.transpose(2, 1, 0, 3, 4).reshape(planes, comps, held_own + new_own, cells)
    own = [own[x] for x in range(planes)]
    place = jnp.stack([lax.axis_index("mode"), lax.axis_index("grid") & 1]).astype(jnp.int32)
    padded = [
        lax.ppermute(own[-1], "grid", shift(count, 1)),
        *own,
        lax.ppermute(own[0], "grid", shift(count, -1)),
    ]
    arrived = gather_planes(own, blocks)
    totals = None
    for x in range(planes):
        last = x == planes - 1
        around = padded[x : x + 3]
        ends = plane_terms(place, *around, arrived[x], totals, last, held_own, new_own, count)
        totals = ends[0]
    keep, send = ends
    sums = keep + lax.ppermute(send, "grid", [(i, i ^ 1) for i in range(count)])
    sums = sums.reshape((2,) * (bits - 1) + (-1, sums.shape[1]))
    middle = sums.shape[-1] // 2 // LANES * LANES
    left = scatter_sum(sums[..., :middle], list(range(1, bits))) * weighting
    right = scatter_sum(sums[..., middle:], list(range(bits - 1, 0, -1))) * weighting
    new_third = new_own * (held_own + new_own) * blocks
    held_third = held_own * new_own * blocks
    rest = new_third + held_third - middle
    return (
        left[:, :new_third],
        jnp.concatenate([left[:, new_third:], right[:, :rest]], 1),
        right[: held_own * blocks // count, rest:],
    )


def solution(mesh):
    placed = (P("mode", None, "grid", None, None), P("mode", None, "grid", None, None))

    def step(held_modes, new_modes):
        body = jax.shard_map(
            per_device,
            mesh=mesh,
            in_specs=placed,
            out_specs=(P("grid", "mode"), P("grid", "mode"), P("grid", "mode")),
            check_vma=False,
        )
        return body(held_modes, new_modes)

    return step
```

profile of v0, /device:TPU:0, one launch (start us, length us, event | category | flops | bytes accessed | tf_op | source)
XLA Modules:
  0.0 128.8 jit_solution(13597355241093861249)
XLA Ops:
  0.6 1.7 %maximum_bitcast_fusion = bf16[4,3,64,4,128]{4,3,0,1,2:T(4,128)(2,1)S(1)} fusion(bf16[8,3,4,4,128]{4,3,2,1,0:T(4,128)(2,1)} %param.3, bf16[56,3,4,4,128]{4,3,2,1,0:T(4,128)(2,1)} %param.2), kind=kLoop, calls=%fused_computation | loop fusion | flops 393216 | bytes 1572864 | tf_op jit(solution)/shard_map/transpose | solution.py:221
  2.7 3.1 %collective-permute-start.11 = (bf16[3,64,512]{2,1,0:T(8,128)(2,1)S(1)}, bf16[3,64,512]{2,1,0:T(8,128)(2,1)S(1)}, u32[]{:S(2)}, u32[]{:S(2)}) collective-permute-start(bf16[3,64,512]{2,1,0:T(8,128)(2,1)S(1)} %squeeze.33.here.rest_0_.before), channel_id=1, source_target_pairs={{0,1},{1,2},{2,3},{3,0},{4,5},{5,6},{6,7},{7,4},{8,9},{9,10},{10,1... | collective-permute-start | bytes 589832 | tf_op jit(solution)/shard_map/ppermute | solution.py:208
  5.9 2.1 %collective-permute-start.13 = (bf16[3,64,512]{2,1,0:T(8,128)(2,1)S(1)}, bf16[3,64,512]{2,1,0:T(8,128)(2,1)S(1)}, u32[]{:S(2)}, u32[]{:S(2)}) collective-permute-start(bf16[3,64,512]{2,1,0:T(8,128)(2,1)S(1)} %squeeze.33.here.rest_0_.before), channel_id=1, source_target_pairs={{0,3},{1,0},{2,1},{3,2},{4,7},{5,4},{6,5},{7,6},{8,11},{9,8},{10,9... | collective-permute-start | bytes 589832 | tf_op jit(solution)/shard_map/ppermute | solution.py:208
  8.4 3.8 %collective-permute-start.9 = (bf16[3,64,512]{2,1,0:T(8,128)(2,1)S(1)}, bf16[3,64,512]{2,1,0:T(8,128)(2,1)S(1)}, u32[]{:S(2)}, u32[]{:S(2)}) collective-permute-start(bf16[3,64,512]{2,1,0:T(8,128)(2,1)S(1)} %squeeze.34.after.here.rest_0_.before), channel_id=1, source_target_pairs={{0,3},{1,0},{2,1},{3,2},{4,7},{5,4},{6,5},{7,6},{8,11},{9,8},{10,9... | collective-permute-start | bytes 589832 | tf_op jit(solution)/shard_map/ppermute | solution.py:208
  12.4 1.3 %collective-permute-done.11.rest_1_ = bf16[3,64,512]{2,1,0:T(8,128)(2,1)S(1)} collective-permute-done((bf16[3,64,512]{2,1,0:T(8,128)(2,1)S(1)}, bf16[3,64,512]{2,1,0:T(8,128)(2,1)S(1)}, u32[]{:S(2)}, u32[]{:S(2)}) %collective-permute-start.11) | collective-permute-done | bytes 196640 | tf_op jit(solution)/shard_map/ppermute | solution.py:208
  13.7 1.8 %collective-permute-start.4 = (bf16[3,64,512]{2,1,0:T(8,128)(2,1)S(1)}, bf16[3,64,512]{2,1,0:T(8,128)(2,1)S(1)}, u32[]{:S(2)}, u32[]{:S(2)}) collective-permute-start(bf16[3,64,512]{2,1,0:T(8,128)(2,1)S(1)} %squeeze.31.after.here.rest_0_.before), channel_id=1, source_target_pairs={{0,1},{1,2},{2,3},{3,0},{4,5},{5,6},{6,7},{7,4},{8,9},{9,10},{10,1... | collective-permute-start | bytes 589832 | tf_op jit(solution)/shard_map/ppermute | solution.py:208
  15.5 3.0 %collective-permute-start.1 = (bf16[3,64,512]{2,1,0:T(8,128)(2,1)S(1)}, bf16[3,64,512]{2,1,0:T(8,128)(2,1)S(1)}, u32[]{:S(2)}, u32[]{:S(2)}) collective-permute-start(bf16[3,64,512]{2,1,0:T(8,128)(2,1)S(1)} %squeeze.32.after.here.rest_0_), channel_id=1, source_target_pairs={{0,1},{1,2},{2,3},{3,0},{4,5},{5,6},{6,7},{7,4},{8,9},{9,10},{10,1... | collective-permute-start | bytes 589832 | tf_op jit(solution)/shard_map/ppermute | solution.py:208
  18.5 1.8 %collective-permute-start.12 = (bf16[3,64,512]{2,1,0:T(8,128)(2,1)S(1)}, bf16[3,64,512]{2,1,0:T(8,128)(2,1)S(1)}, u32[]{:S(2)}, u32[]{:S(2)}) collective-permute-start(bf16[3,64,512]{2,1,0:T(8,128)(2,1)S(1)} %collective-permute-done.11.rest_1_), channel_id=1, source_target_pairs={{0,1},{1,2},{2,3},{3,0},{4,5},{5,6},{6,7},{7,4},{8,9},{9,10},{10,1... | collective-permute-start | bytes 589832 | tf_op jit(solution)/shard_map/ppermute | solution.py:208
  20.2 1.9 %collective-permute-done.7.rest_1_ = bf16[3,64,512]{2,1,0:T(8,128)(2,1)S(1)} collective-permute-done((bf16[3,64,512]{2,1,0:T(8,128)(2,1)S(1)}, bf16[3,64,512]{2,1,0:T(8,128)(2,1)S(1)}, u32[]{:S(2)}, u32[]{:S(2)}) %collective-permute-start.7) | collective-permute-done | bytes 196640 | tf_op jit(solution)/shard_map/ppermute | solution.py:208
  22.1 1.7 %collective-permute-start.8 = (bf16[3,64,512]{2,1,0:T(8,128)(2,1)S(1)}, bf16[3,64,512]{2,1,0:T(8,128)(2,1)S(1)}, u32[]{:S(2)}, u32[]{:S(2)}) collective-permute-start(bf16[3,64,512]{2,1,0:T(8,128)(2,1)S(1)} %collective-permute-done.7.rest_1_), channel_id=1, source_target_pairs={{0,1},{1,2},{2,3},{3,0},{4,5},{5,6},{6,7},{7,4},{8,9},{9,10},{10,1... | collective-permute-start | bytes 589832 | tf_op jit(solution)/shard_map/ppermute | solution.py:208
  23.9 1.2 collective-permute-done.9.rest_3_
  25.1 3.1 %collective-permute-start.6 = (bf16[3,64,512]{2,1,0:T(8,128)(2,1)S(1)}, bf16[3,64,512]{2,1,0:T(8,128)(2,1)S(1)}, u32[]{:S(2)}, u32[]{:S(2)}) collective-permute-start(bf16[3,64,512]{2,1,0:T(8,128)(2,1)S(1)} %squeeze.31.after.here.rest_0_.before), channel_id=1, source_target_pairs={{0,3},{1,0},{2,1},{3,2},{4,7},{5,4},{6,5},{7,6},{8,11},{9,8},{10,9... | collective-permute-start | bytes 589832 | tf_op jit(solution)/shard_map/ppermute | solution.py:208
  28.2 2.5 %collective-permute-done.4.rest_1_ = bf16[3,64,512]{2,1,0:T(8,128)(2,1)S(1)} collective-permute-done((bf16[3,64,512]{2,1,0:T(8,128)(2,1)S(1)}, bf16[3,64,512]{2,1,0:T(8,128)(2,1)S(1)}, u32[]{:S(2)}, u32[]{:S(2)}) %collective-permute-start.4) | collective-permute-done | bytes 196640 | tf_op jit(solution)/shard_map/ppermute | solution.py:208
  30.8 4.1 %collective-permute-done.1.rest_1_ = bf16[3,64,512]{2,1,0:T(8,128)(2,1)S(1)} collective-permute-done((bf16[3,64,512]{2,1,0:T(8,128)(2,1)S(1)}, bf16[3,64,512]{2,1,0:T(8,128)(2,1)S(1)}, u32[]{:S(2)}, u32[]{:S(2)}) %collective-permute-start.1) | collective-permute-done | bytes 196640 | tf_op jit(solution)/shard_map/ppermute | solution.py:208
  34.9 4.2 %collective-permute-done.12.rest_2_ = bf16[3,64,512]{2,1,0:T(8,128)(2,1)S(1)} collective-permute-done((bf16[3,64,512]{2,1,0:T(8,128)(2,1)S(1)}, bf16[3,64,512]{2,1,0:T(8,128)(2,1)S(1)}, u32[]{:S(2)}, u32[]{:S(2)}) %collective-permute-start.12) | collective-permute-done | bytes 196640 | tf_op jit(solution)/shard_map/ppermute | solution.py:208
  39.1 1.4 %collective-permute-start.3 = (bf16[3,64,512]{2,1,0:T(8,128)(2,1)S(1)}, bf16[3,64,512]{2,1,0:T(8,128)(2,1)S(1)}, u32[]{:S(2)}, u32[]{:S(2)}) collective-permute-start(bf16[3,64,512]{2,1,0:T(8,128)(2,1)S(1)} %squeeze.32.after.here.rest_0_), channel_id=1, source_target_pairs={{0,3},{1,0},{2,1},{3,2},{4,7},{5,4},{6,5},{7,6},{8,11},{9,8},{10,9... | collective-permute-start | bytes 589832 | tf_op jit(solution)/shard_map/ppermute | solution.py:208
  40.5 2.8 %collective-permute-done.8.rest_2_ = bf16[3,64,512]{2,1,0:T(8,128)(2,1)S(1)} collective-permute-done((bf16[3,64,512]{2,1,0:T(8,128)(2,1)S(1)}, bf16[3,64,512]{2,1,0:T(8,128)(2,1)S(1)}, u32[]{:S(2)}, u32[]{:S(2)}) %collective-permute-start.8) | collective-permute-done | bytes 196640 | tf_op jit(solution)/shard_map/ppermute | solution.py:208
  43.3 1.6 %collective-permute-start.2 = (bf16[3,64,512]{2,1,0:T(8,128)(2,1)S(1)}, bf16[3,64,512]{2,1,0:T(8,128)(2,1)S(1)}, u32[]{:S(2)}, u32[]{:S(2)}) collective-permute-start(bf16[3,64,512]{2,1,0:T(8,128)(2,1)S(1)} %collective-permute-done.1.rest_1_), channel_id=1, source_target_pairs={{0,1},{1,2},{2,3},{3,0},{4,5},{5,6},{6,7},{7,4},{8,9},{9,10},{10,1... | collective-permute-start | bytes 589832 | tf_op jit(solution)/shard_map/ppermute | solution.py:208
  45.0 11.9 %plane_terms.4.rest_4_ = f32[256,5632]{1,0:T(8,128)S(1)} custom-call(s32[2]{0:T(128)S(1)} %pad_add_fusion.me_ref, bf16[3,64,512]{2,1,0:T(8,128)(2,1)S(1)} %collective-permute-done.10.before, bf16[3,64,512]{2,1,0:T(8,128)(2,1)S(1)} %squeeze.33.here.rest_0_.before, bf16[3,64,512]{2,1,0:T(8,128)(2,1)S(1)} %squeeze.34.after.here.rest_0_.before, ...), custom_call_target="tpu_custom_call" | custom-call | tf_op jit(solution)/shard_map/plane_terms/pallas_call | solution.py:166
  56.9 12.0 %plane_terms.5.rest_4_ = f32[256,5632]{1,0:T(8,128)S(1)} custom-call(s32[2]{0:T(128)S(1)} %pad_add_fusion.me_ref, bf16[3,64,512]{2,1,0:T(8,128)(2,1)S(1)} %squeeze.33.here.rest_0_.before, bf16[3,64,512]{2,1,0:T(8,128)(2,1)S(1)} %squeeze.34.after.here.rest_0_.before, ...), custom_call_target="tpu_custom_call", output_to_operand_aliasing={{}: (8, {})} | custom-call | tf_op jit(solution)/shard_map/plane_terms/pallas_call | solution.py:166
  68.9 12.0 %plane_terms.6.rest_4_ = f32[256,5632]{1,0:T(8,128)S(1)} custom-call(s32[2]{0:T(128)S(1)} %pad_add_fusion.me_ref, bf16[3,64,512]{2,1,0:T(8,128)(2,1)S(1)} %squeeze.34.after.here.rest_0_.before, bf16[3,64,512]{2,1,0:T(8,128)(2,1)S(1)} %squeeze.31.after.here.rest_0_.before, ...), custom_call_target="tpu_custom_call", output_to_operand_aliasing={{}: (8, {})} | custom-call | tf_op jit(solution)/shard_map/plane_terms/pallas_call | solution.py:166
  83.0 0.9 copy-done.3
  85.8 13.5 %plane_terms.7 = (f32[128,5632]{1,0:T(8,128)S(1)}, f32[128,5632]{1,0:T(8,128)}) custom-call(s32[2]{0:T(128)S(1)} %pad_add_fusion.me_ref, bf16[3,64,512]{2,1,0:T(8,128)(2,1)S(1)} %squeeze.31.after.here.rest_0_.before, bf16[3,64,512]{2,1,0:T(8,128)(2,1)S(1)} %squeeze.32.after.here.rest_0_, bf16[3,64,512]{2,1,0:T(8,128)(2,1)S(1)} %copy-done.3, ...), custom_call_target="tpu_custom_call" | custom-call | tf_op jit(solution)/shard_map/plane_terms/pallas_call | solution.py:166
  99.3 5.6 %collective-permute-done.14 = f32[128,5632]{1,0:T(8,128)} collective-permute-done((f32[128,5632]{1,0:T(8,128)}, f32[128,5632]{1,0:T(8,128)}, u32[]{:S(2)}, u32[]{:S(2)}) %collective-permute-start.14) | collective-permute-done | bytes 2883616 | tf_op jit(solution)/shard_map/ppermute | solution.py:237
  104.9 2.1 %add.36 = f32[128,5632]{1,0:T(8,128)S(1)} add(f32[128,5632]{1,0:T(8,128)S(1)} %get-tuple-element.5, f32[128,5632]{1,0:T(8,128)} %collective-permute-done.14) | non-fusion elementwise | flops 720896 | bytes 8650752 | tf_op jit(solution)/shard_map/add | solution.py:237
  107.4 1.6 %collective-permute-start.17 = (bf16[2,32,2816]{2,1,0:T(8,128)(2,1)S(1)}, bf16[2,32,2816]{2,1,0:T(8,128)(2,1)}, u32[]{:S(2)}, u32[]{:S(2)}) collective-permute-start(bf16[2,32,2816]{2,1,0:T(8,128)(2,1)S(1)} %fusion), channel_id=1, source_target_pairs={{0,16},{4,20},{8,24},{12,28},{16,0},{20,4},{24,8},{28,12},{1,17},{... | collective-permute-start | bytes 1081352 | tf_op jit(solution)/shard_map/ppermute | solution.py:197
  109.0 2.6 %collective-permute-start.15 = (bf16[2,32,2816]{2,1,0:T(8,128)(2,1)S(1)}, bf16[2,32,2816]{2,1,0:T(8,128)(2,1)S(1)}, u32[]{:S(2)}, u32[]{:S(2)}) collective-permute-start(bf16[2,32,2816]{2,1,0:T(8,128)(2,1)S(1)} %fusion.1), channel_id=1, source_target_pairs={{0,8},{4,12},{8,0},{12,4},{16,24},{20,28},{24,16},{28,20},{1,9},{5... | collective-permute-start | bytes 1081352 | tf_op jit(solution)/shard_map/ppermute | solution.py:197
  111.6 6.4 %collective-permute-done.17 = bf16[2,32,2816]{2,1,0:T(8,128)(2,1)} collective-permute-done((bf16[2,32,2816]{2,1,0:T(8,128)(2,1)S(1)}, bf16[2,32,2816]{2,1,0:T(8,128)(2,1)}, u32[]{:S(2)}, u32[]{:S(2)}) %collective-permute-start.17) | collective-permute-done | bytes 360480 | tf_op jit(solution)/shard_map/ppermute | solution.py:197
  118.0 1.0 bitcast_add_fusion.1
  119.1 2.4 %collective-permute-start.18 = (bf16[32,2816]{1,0:T(8,128)(2,1)S(1)}, bf16[32,2816]{1,0:T(8,128)(2,1)S(1)}, u32[]{:S(2)}, u32[]{:S(2)}) collective-permute-start(bf16[32,2816]{1,0:T(8,128)(2,1)S(1)} %fusion.5), channel_id=1, source_target_pairs={{0,8},{4,12},{8,0},{12,4},{16,24},{20,28},{24,16},{28,20},{1,9},{5... | collective-permute-start | bytes 540680 | tf_op jit(solution)/shard_map/ppermute | solution.py:197
  121.5 1.8 %collective-permute-start.16 = (bf16[32,2816]{1,0:T(8,128)(2,1)S(1)}, bf16[32,2816]{1,0:T(8,128)(2,1)S(1)}, u32[]{:S(2)}, u32[]{:S(2)}) collective-permute-start(bf16[32,2816]{1,0:T(8,128)(2,1)S(1)} %fusion.4), channel_id=1, source_target_pairs={{0,16},{4,20},{8,24},{12,28},{16,0},{20,4},{24,8},{28,12},{1,17},{... | collective-permute-start | bytes 540680 | tf_op jit(solution)/shard_map/ppermute | solution.py:197
  123.3 2.4 %collective-permute-done.18 = bf16[32,2816]{1,0:T(8,128)(2,1)S(1)} collective-permute-done((bf16[32,2816]{1,0:T(8,128)(2,1)S(1)}, bf16[32,2816]{1,0:T(8,128)(2,1)S(1)}, u32[]{:S(2)}, u32[]{:S(2)}) %collective-permute-start.18) | collective-permute-done | bytes 180256 | tf_op jit(solution)/shard_map/ppermute | solution.py:197
  (52 shorter events, 8.7 us)
Async XLA Ops:
  2.7 10.9 %collective-permute-start.11 = (bf16[3,64,512]{2,1,0:T(8,128)(2,1)S(1)}, bf16[3,64,512]{2,1,0:T(8,128)(2,1)S(1)}, u32[]{:S(2)}, u32[]{:S(2)}) collective-permute-start(bf16[3,64,512]{2,1,0:T(8,128)(2,1)S(1)} %squeeze.33.here.rest_0_.before), channel_id=1, source_target_pairs={{0,1},{1,2},{2,3},{3,0},{4,5},{5,6},{6,7},{7,4},{8,9},{9,10},{10,1... | collective-permute-start | bytes 589832 | tf_op jit(solution)/shard_map/ppermute | solution.py:208
  5.9 12.6 %collective-permute-start.13 = (bf16[3,64,512]{2,1,0:T(8,128)(2,1)S(1)}, bf16[3,64,512]{2,1,0:T(8,128)(2,1)S(1)}, u32[]{:S(2)}, u32[]{:S(2)}) collective-permute-start(bf16[3,64,512]{2,1,0:T(8,128)(2,1)S(1)} %squeeze.33.here.rest_0_.before), channel_id=1, source_target_pairs={{0,3},{1,0},{2,1},{3,2},{4,7},{5,4},{6,5},{7,6},{8,11},{9,8},{10,9... | collective-permute-start | bytes 589832 | tf_op jit(solution)/shard_map/ppermute | solution.py:208
  8.1 7.4 %collective-permute-start.10 = (bf16[3,64,512]{2,1,0:T(8,128)(2,1)S(1)}, bf16[3,64,512]{2,1,0:T(8,128)(2,1)S(1)}, u32[]{:S(2)}, u32[]{:S(2)}) collective-permute-start(bf16[3,64,512]{2,1,0:T(8,128)(2,1)S(1)} %squeeze.32.after.here.rest_0_), channel_id=1, source_target_pairs={{0,4},{4,8},{8,12},{12,16},{16,20},{20,24},{24,28},{28,0},{1,5},{5... | collective-permute-start | bytes 589832 | tf_op jit(solution)/shard_map/ppermute | solution.py:225
  8.3 13.8 %collective-permute-start.7 = (bf16[3,64,512]{2,1,0:T(8,128)(2,1)S(1)}, bf16[3,64,512]{2,1,0:T(8,128)(2,1)S(1)}, u32[]{:S(2)}, u32[]{:S(2)}) collective-permute-start(bf16[3,64,512]{2,1,0:T(8,128)(2,1)S(1)} %squeeze.34.after.here.rest_0_.before), channel_id=1, source_target_pairs={{0,1},{1,2},{2,3},{3,0},{4,5},{5,6},{6,7},{7,4},{8,9},{9,10},{10,1... | collective-permute-start | bytes 589832 | tf_op jit(solution)/shard_map/ppermute | solution.py:208
  8.4 16.7 %collective-permute-start.9 = (bf16[3,64,512]{2,1,0:T(8,128)(2,1)S(1)}, bf16[3,64,512]{2,1,0:T(8,128)(2,1)S(1)}, u32[]{:S(2)}, u32[]{:S(2)}) collective-permute-start(bf16[3,64,512]{2,1,0:T(8,128)(2,1)S(1)} %squeeze.34.after.here.rest_0_.before), channel_id=1, source_target_pairs={{0,3},{1,0},{2,1},{3,2},{4,7},{5,4},{6,5},{7,6},{8,11},{9,8},{10,9... | collective-permute-start | bytes 589832 | tf_op jit(solution)/shard_map/ppermute | solution.py:208
  13.7 17.0 %collective-permute-start.4 = (bf16[3,64,512]{2,1,0:T(8,128)(2,1)S(1)}, bf16[3,64,512]{2,1,0:T(8,128)(2,1)S(1)}, u32[]{:S(2)}, u32[]{:S(2)}) collective-permute-start(bf16[3,64,512]{2,1,0:T(8,128)(2,1)S(1)} %squeeze.31.after.here.rest_0_.before), channel_id=1, source_target_pairs={{0,1},{1,2},{2,3},{3,0},{4,5},{5,6},{6,7},{7,4},{8,9},{9,10},{10,1... | collective-permute-start | bytes 589832 | tf_op jit(solution)/shard_map/ppermute | solution.py:208
  15.5 19.4 %collective-permute-start.1 = (bf16[3,64,512]{2,1,0:T(8,128)(2,1)S(1)}, bf16[3,64,512]{2,1,0:T(8,128)(2,1)S(1)}, u32[]{:S(2)}, u32[]{:S(2)}) collective-permute-start(bf16[3,64,512]{2,1,0:T(8,128)(2,1)S(1)} %squeeze.32.after.here.rest_0_), channel_id=1, source_target_pairs={{0,1},{1,2},{2,3},{3,0},{4,5},{5,6},{6,7},{7,4},{8,9},{9,10},{10,1... | collective-permute-start | bytes 589832 | tf_op jit(solution)/shard_map/ppermute | solution.py:208
  18.5 20.6 %collective-permute-start.12 = (bf16[3,64,512]{2,1,0:T(8,128)(2,1)S(1)}, bf16[3,64,512]{2,1,0:T(8,128)(2,1)S(1)}, u32[]{:S(2)}, u32[]{:S(2)}) collective-permute-start(bf16[3,64,512]{2,1,0:T(8,128)(2,1)S(1)} %collective-permute-done.11.rest_1_), channel_id=1, source_target_pairs={{0,1},{1,2},{2,3},{3,0},{4,5},{5,6},{6,7},{7,4},{8,9},{9,10},{10,1... | collective-permute-start | bytes 589832 | tf_op jit(solution)/shard_map/ppermute | solution.py:208
  22.1 21.1 %collective-permute-start.8 = (bf16[3,64,512]{2,1,0:T(8,128)(2,1)S(1)}, bf16[3,64,512]{2,1,0:T(8,128)(2,1)S(1)}, u32[]{:S(2)}, u32[]{:S(2)}) collective-permute-start(bf16[3,64,512]{2,1,0:T(8,128)(2,1)S(1)} %collective-permute-done.7.rest_1_), channel_id=1, source_target_pairs={{0,1},{1,2},{2,3},{3,0},{4,5},{5,6},{6,7},{7,4},{8,9},{9,10},{10,1... | collective-permute-start | bytes 589832 | tf_op jit(solution)/shard_map/ppermute | solution.py:208
  25.1 43.9 %collective-permute-start.6 = (bf16[3,64,512]{2,1,0:T(8,128)(2,1)S(1)}, bf16[3,64,512]{2,1,0:T(8,128)(2,1)S(1)}, u32[]{:S(2)}, u32[]{:S(2)}) collective-permute-start(bf16[3,64,512]{2,1,0:T(8,128)(2,1)S(1)} %squeeze.31.after.here.rest_0_.before), channel_id=1, source_target_pairs={{0,3},{1,0},{2,1},{3,2},{4,7},{5,4},{6,5},{7,6},{8,11},{9,8},{10,9... | collective-permute-start | bytes 589832 | tf_op jit(solution)/shard_map/ppermute | solution.py:208
  30.7 50.3 %collective-permute-start = (bf16[3,64,512]{2,1,0:T(8,128)(2,1)S(1)}, bf16[3,64,512]{2,1,0:T(8,128)(2,1)S(1)}, u32[]{:S(2)}, u32[]{:S(2)}) collective-permute-start(bf16[3,64,512]{2,1,0:T(8,128)(2,1)S(1)} %squeeze.33.here.rest_0_.before), channel_id=1, source_target_pairs={{0,28},{4,0},{8,4},{12,8},{16,12},{20,16},{24,20},{28,24},{1,29},{... | collective-permute-start | bytes 589832 | tf_op jit(solution)/shard_map/ppermute | solution.py:227
  34.9 22.0 %copy-start = (bf16[3,64,512]{2,1,0:T(8,128)(2,1)}, bf16[3,64,512]{2,1,0:T(8,128)(2,1)S(1)}, u32[]{:S(2)}) copy-start(bf16[3,64,512]{2,1,0:T(8,128)(2,1)S(1)} %collective-permute-done.1.rest_1_) | copy-start | bytes 589828
  34.9 34.0 %collective-permute-start.5 = (bf16[3,64,512]{2,1,0:T(8,128)(2,1)S(1)}, bf16[3,64,512]{2,1,0:T(8,128)(2,1)S(1)}, u32[]{:S(2)}, u32[]{:S(2)}) collective-permute-start(bf16[3,64,512]{2,1,0:T(8,128)(2,1)S(1)} %collective-permute-done.4.rest_1_), channel_id=1, source_target_pairs={{0,1},{1,2},{2,3},{3,0},{4,5},{5,6},{6,7},{7,4},{8,9},{9,10},{10,1... | collective-permute-start | bytes 589832 | tf_op jit(solution)/shard_map/ppermute | solution.py:208
  39.1 42.5 %collective-permute-start.3 = (bf16[3,64,512]{2,1,0:T(8,128)(2,1)S(1)}, bf16[3,64,512]{2,1,0:T(8,128)(2,1)S(1)}, u32[]{:S(2)}, u32[]{:S(2)}) collective-permute-start(bf16[3,64,512]{2,1,0:T(8,128)(2,1)S(1)} %squeeze.32.after.here.rest_0_), channel_id=1, source_target_pairs={{0,3},{1,0},{2,1},{3,2},{4,7},{5,4},{6,5},{7,6},{8,11},{9,8},{10,9... | collective-permute-start | bytes 589832 | tf_op jit(solution)/shard_map/ppermute | solution.py:208
  43.3 39.1 %collective-permute-start.2 = (bf16[3,64,512]{2,1,0:T(8,128)(2,1)S(1)}, bf16[3,64,512]{2,1,0:T(8,128)(2,1)S(1)}, u32[]{:S(2)}, u32[]{:S(2)}) collective-permute-start(bf16[3,64,512]{2,1,0:T(8,128)(2,1)S(1)} %collective-permute-done.1.rest_1_), channel_id=1, source_target_pairs={{0,1},{1,2},{2,3},{3,0},{4,5},{5,6},{6,7},{7,4},{8,9},{9,10},{10,1... | collective-permute-start | bytes 589832 | tf_op jit(solution)/shard_map/ppermute | solution.py:208
  68.9 14.1 %copy-start.1 = (bf16[3,64,512]{2,1,0:T(8,128)(2,1)S(1)}, bf16[3,64,512]{2,1,0:T(8,128)(2,1)}, u32[]{:S(2)}) copy-start(bf16[3,64,512]{2,1,0:T(8,128)(2,1)} %copy-done) | copy-start | bytes 589828
  80.9 0.7 copy-start.2
  81.6 0.7 copy-start.4
  82.3 0.7 copy-start.6
  83.0 0.9 copy-start.3
  83.9 0.9 copy-start.5
  84.8 0.9 copy-start.7
  99.3 5.6 %collective-permute-start.14 = (f32[128,5632]{1,0:T(8,128)}, f32[128,5632]{1,0:T(8,128)}, u32[]{:S(2)}, u32[]{:S(2)}) collective-permute-start(f32[128,5632]{1,0:T(8,128)} %get-tuple-element.6), channel_id=1, source_target_pairs={{0,4},{4,0},{8,12},{12,8},{16,20},{20,16},{24,28},{28,24},{1,5},{5... | collective-permute-start | bytes 8650760 | tf_op jit(solution)/shard_map/ppermute | solution.py:237
  107.4 10.6 %collective-permute-start.17 = (bf16[2,32,2816]{2,1,0:T(8,128)(2,1)S(1)}, bf16[2,32,2816]{2,1,0:T(8,128)(2,1)}, u32[]{:S(2)}, u32[]{:S(2)}) collective-permute-start(bf16[2,32,2816]{2,1,0:T(8,128)(2,1)S(1)} %fusion), channel_id=1, source_target_pairs={{0,16},{4,20},{8,24},{12,28},{16,0},{20,4},{24,8},{28,12},{1,17},{... | collective-permute-start | bytes 1081352 | tf_op jit(solution)/shard_map/ppermute | solution.py:197
  109.0 12.4 %collective-permute-start.15 = (bf16[2,32,2816]{2,1,0:T(8,128)(2,1)S(1)}, bf16[2,32,2816]{2,1,0:T(8,128)(2,1)S(1)}, u32[]{:S(2)}, u32[]{:S(2)}) collective-permute-start(bf16[2,32,2816]{2,1,0:T(8,128)(2,1)S(1)} %fusion.1), channel_id=1, source_target_pairs={{0,8},{4,12},{8,0},{12,4},{16,24},{20,28},{24,16},{28,20},{1,9},{5... | collective-permute-start | bytes 1081352 | tf_op jit(solution)/shard_map/ppermute | solution.py:197
  119.1 6.6 %collective-permute-start.18 = (bf16[32,2816]{1,0:T(8,128)(2,1)S(1)}, bf16[32,2816]{1,0:T(8,128)(2,1)S(1)}, u32[]{:S(2)}, u32[]{:S(2)}) collective-permute-start(bf16[32,2816]{1,0:T(8,128)(2,1)S(1)} %fusion.5), channel_id=1, source_target_pairs={{0,8},{4,12},{8,0},{12,4},{16,24},{20,28},{24,16},{28,20},{1,9},{5... | collective-permute-start | bytes 540680 | tf_op jit(solution)/shard_map/ppermute | solution.py:197
  121.5 5.8 %collective-permute-start.16 = (bf16[32,2816]{1,0:T(8,128)(2,1)S(1)}, bf16[32,2816]{1,0:T(8,128)(2,1)S(1)}, u32[]{:S(2)}, u32[]{:S(2)}) collective-permute-start(bf16[32,2816]{1,0:T(8,128)(2,1)S(1)} %fusion.4), channel_id=1, source_target_pairs={{0,16},{4,20},{8,24},{12,28},{16,0},{20,4},{24,8},{28,12},{1,17},{... | collective-permute-start | bytes 540680 | tf_op jit(solution)/shard_map/ppermute | solution.py:197
where the time goes:
time: 129 us
  Pallas kernels  49.5 us (38%)
  waiting for transfers between devices  33.3 us (26%)
  starting transfers between devices  32 us (25%)
  local copies, waits for them, and re-layouts  7.52 us (6%)
  other arithmetic  5.75 us (4%)
    pallas_call x4, Pallas kernels, plane_terms(): pl.pallas_call(functools.partial(plane_kernel, totals is None, last, held...  49.5 us
    ppermute x12, starting transfers between devices, gather_planes(): lax.ppermute(source, 'mode', shift(blocks, -1 if straight else 1))  23.4 us
    ppermute x12, waiting for transfers between devices, gather_planes(): lax.ppermute(source, 'mode', shift(blocks, -1 if straight else 1))  18 us
    ppermute x4, waiting for transfers between devices, scatter_sum(): lax.ppermute(send, 'grid', [(i, i ^ 1 << bit) for i in range(count)])  9.65 us
    ppermute x4, starting transfers between devices, scatter_sum(): lax.ppermute(send, 'grid', [(i, i ^ 1 << bit) for i in range(count)])  8.33 us
    ppermute x1, waiting for transfers between devices, per_device(): sums = keep + lax.ppermute(send, 'grid', [(i, i ^ 1) for i in range(count)])  5.62 us
    unnamed x16, local copies, waits for them, and re-layouts  4.82 us
  transfers between devices with their start and end apart: 19, of which 11 were waited for; matrix products, arithmetic and copies ran while one was open for 2% of the time, Pallas kernels for 28%

commit v1 on v0

--- a/solution.py
+++ b/solution.py
@@ -119,7 +119,7 @@
         columns = pl.ds(pl.multiple_of(tile * total, LANES), total)
         value = value if first else totals[:, columns] + value
         for i, out in enumerate(outs):
-            out[:, columns] = value[i * half : (i + 1) * half] if last else value
+            out[:, columns] = value[i * half : (i + 1) * half].astype(out.dtype) if last else value
 
     def one(step, carry):
         @pl.when(step == 0)
@@ -165,7 +165,7 @@
     rows = [total // 2] * 2 if last else [total]
     return pl.pallas_call(
         functools.partial(plane_kernel, totals is None, last, held_own, new_own, owners, blocks),
-        out_shape=[jax.ShapeDtypeStruct((n, columns), F32) for n in rows],
+        out_shape=[jax.ShapeDtypeStruct((n, columns), t) for n, t in zip(rows, (F32, BF16))],
         in_specs=[pl.BlockSpec(memory_space=pltpu.SMEM)] + [vmem] * (len(operands) - 1),
         out_specs=[vmem] * len(rows),
         scratch_shapes=[
@@ -234,7 +234,7 @@
         ends = plane_terms(place, *around, arrived[x], totals, last, held_own, new_own, count)
         totals = ends[0]
     keep, send = ends
-    sums = keep + lax.ppermute(send, "grid", [(i, i ^ 1) for i in range(count)])
+    sums = keep + lax.ppermute(send, "grid", [(i, i ^ 1) for i in range(count)]).astype(F32)
     sums = sums.reshape((2,) * (bits - 1) + (-1, sums.shape[1]))
     middle = sums.shape[-1] // 2 // LANES * LANES
     left = scatter_sum(sums[..., :middle], list(range(1, bits))) * weighting

time: 129 us -> 126 us (0.977)
  waiting for transfers between devices: 33.3 us -> 31.2 us
    ppermute x1, waiting for transfers between devices: 5.62 us -> 3.56 us  [per_device(): lax.ppermute(send, 'grid', [(i, i ^ 1) for i in range(count)]).astype(F32)]
  transfers between devices with their start and end apart: 19 -> 19, of which waited for: 11 -> 11; matrix products, arithmetic and copies ran while one was open for 2% -> 2% of each run, Pallas kernels for 28% -> 29%
where the time goes in v1:
time: 126 us
  Pallas kernels  49 us (39%)
  starting transfers between devices  32 us (25%)
  waiting for transfers between devices  31.2 us (25%)
  local copies, waits for them, and re-layouts  7.51 us (6%)
  other arithmetic  5.26 us (4%)
    pallas_call x4, Pallas kernels, plane_terms(): pl.pallas_call(functools.partial(plane_kernel, totals is None, last, held...  49 us
    ppermute x12, starting transfers between devices, gather_planes(): lax.ppermute(source, 'mode', shift(blocks, -1 if straight else 1))  23.4 us
    ppermute x12, waiting for transfers between devices, gather_planes(): lax.ppermute(source, 'mode', shift(blocks, -1 if straight else 1))  18 us
    ppermute x4, waiting for transfers between devices, scatter_sum(): lax.ppermute(send, 'grid', [(i, i ^ 1 << bit) for i in range(count)])  9.65 us
    ppermute x4, starting transfers between devices, scatter_sum(): lax.ppermute(send, 'grid', [(i, i ^ 1 << bit) for i in range(count)])  8.33 us
    unnamed x16, local copies, waits for them, and re-layouts  4.82 us
    ppermute x1, waiting for transfers between devices, per_device(): lax.ppermute(send, 'grid', [(i, i ^ 1) for i in range(count)]).astype(F32)  3.56 us
  transfers between devices with their start and end apart: 19, of which 11 were waited for; matrix products, arithmetic and copies ran while one was open for 2% of the time, Pallas kernels for 29%

profile of v1, /device:TPU:0, one launch (start us, length us, event | category | flops | bytes accessed | tf_op | source)
XLA Modules:
  0.0 125.8 jit_solution(8528755370661203891)
XLA Ops:
  0.6 1.7 %maximum_bitcast_fusion = bf16[4,3,64,4,128]{4,3,0,1,2:T(4,128)(2,1)S(1)} fusion(bf16[8,3,4,4,128]{4,3,2,1,0:T(4,128)(2,1)} %param.3, bf16[56,3,4,4,128]{4,3,2,1,0:T(4,128)(2,1)} %param.2), kind=kLoop, calls=%fused_computation.1 | loop fusion | flops 393216 | bytes 1572864 | tf_op jit(solution)/shard_map/transpose | solution.py:221
  2.7 3.1 %collective-permute-start.11 = (bf16[3,64,512]{2,1,0:T(8,128)(2,1)S(1)}, bf16[3,64,512]{2,1,0:T(8,128)(2,1)S(1)}, u32[]{:S(2)}, u32[]{:S(2)}) collective-permute-start(bf16[3,64,512]{2,1,0:T(8,128)(2,1)S(1)} %squeeze.33.here.rest_0_.before), channel_id=1, source_target_pairs={{0,1},{1,2},{2,3},{3,0},{4,5},{5,6},{6,7},{7,4},{8,9},{9,10},{10,1... | collective-permute-start | bytes 589832 | tf_op jit(solution)/shard_map/ppermute | solution.py:208
  5.9 2.1 %collective-permute-start.13 = (bf16[3,64,512]{2,1,0:T(8,128)(2,1)S(1)}, bf16[3,64,512]{2,1,0:T(8,128)(2,1)S(1)}, u32[]{:S(2)}, u32[]{:S(2)}) collective-permute-start(bf16[3,64,512]{2,1,0:T(8,128)(2,1)S(1)} %squeeze.33.here.rest_0_.before), channel_id=1, source_target_pairs={{0,3},{1,0},{2,1},{3,2},{4,7},{5,4},{6,5},{7,6},{8,11},{9,8},{10,9... | collective-permute-start | bytes 589832 | tf_op jit(solution)/shard_map/ppermute | solution.py:208
  8.4 3.8 %collective-permute-start.9 = (bf16[3,64,512]{2,1,0:T(8,128)(2,1)S(1)}, bf16[3,64,512]{2,1,0:T(8,128)(2,1)S(1)}, u32[]{:S(2)}, u32[]{:S(2)}) collective-permute-start(bf16[3,64,512]{2,1,0:T(8,128)(2,1)S(1)} %squeeze.34.after.here.rest_0_.before), channel_id=1, source_target_pairs={{0,3},{1,0},{2,1},{3,2},{4,7},{5,4},{6,5},{7,6},{8,11},{9,8},{10,9... | collective-permute-start | bytes 589832 | tf_op jit(solution)/shard_map/ppermute | solution.py:208
  12.4 1.3 %collective-permute-done.11.rest_1_ = bf16[3,64,512]{2,1,0:T(8,128)(2,1)S(1)} collective-permute-done((bf16[3,64,512]{2,1,0:T(8,128)(2,1)S(1)}, bf16[3,64,512]{2,1,0:T(8,128)(2,1)S(1)}, u32[]{:S(2)}, u32[]{:S(2)}) %collective-permute-start.11) | collective-permute-done | bytes 196640 | tf_op jit(solution)/shard_map/ppermute | solution.py:208
  13.7 1.8 %collective-permute-start.4 = (bf16[3,64,512]{2,1,0:T(8,128)(2,1)S(1)}, bf16[3,64,512]{2,1,0:T(8,128)(2,1)S(1)}, u32[]{:S(2)}, u32[]{:S(2)}) collective-permute-start(bf16[3,64,512]{2,1,0:T(8,128)(2,1)S(1)} %squeeze.31.after.here.rest_0_.before), channel_id=1, source_target_pairs={{0,1},{1,2},{2,3},{3,0},{4,5},{5,6},{6,7},{7,4},{8,9},{9,10},{10,1... | collective-permute-start | bytes 589832 | tf_op jit(solution)/shard_map/ppermute | solution.py:208
  15.5 3.0 %collective-permute-start.1 = (bf16[3,64,512]{2,1,0:T(8,128)(2,1)S(1)}, bf16[3,64,512]{2,1,0:T(8,128)(2,1)S(1)}, u32[]{:S(2)}, u32[]{:S(2)}) collective-permute-start(bf16[3,64,512]{2,1,0:T(8,128)(2,1)S(1)} %squeeze.32.after.here.rest_0_), channel_id=1, source_target_pairs={{0,1},{1,2},{2,3},{3,0},{4,5},{5,6},{6,7},{7,4},{8,9},{9,10},{10,1... | collective-permute-start | bytes 589832 | tf_op jit(solution)/shard_map/ppermute | solution.py:208
  18.5 1.8 %collective-permute-start.12 = (bf16[3,64,512]{2,1,0:T(8,128)(2,1)S(1)}, bf16[3,64,512]{2,1,0:T(8,128)(2,1)S(1)}, u32[]{:S(2)}, u32[]{:S(2)}) collective-permute-start(bf16[3,64,512]{2,1,0:T(8,128)(2,1)S(1)} %collective-permute-done.11.rest_1_), channel_id=1, source_target_pairs={{0,1},{1,2},{2,3},{3,0},{4,5},{5,6},{6,7},{7,4},{8,9},{9,10},{10,1... | collective-permute-start | bytes 589832 | tf_op jit(solution)/shard_map/ppermute | solution.py:208
  20.2 1.9 %collective-permute-done.7.rest_1_ = bf16[3,64,512]{2,1,0:T(8,128)(2,1)S(1)} collective-permute-done((bf16[3,64,512]{2,1,0:T(8,128)(2,1)S(1)}, bf16[3,64,512]{2,1,0:T(8,128)(2,1)S(1)}, u32[]{:S(2)}, u32[]{:S(2)}) %collective-permute-start.7) | collective-permute-done | bytes 196640 | tf_op jit(solution)/shard_map/ppermute | solution.py:208
  22.1 1.7 %collective-permute-start.8 = (bf16[3,64,512]{2,1,0:T(8,128)(2,1)S(1)}, bf16[3,64,512]{2,1,0:T(8,128)(2,1)S(1)}, u32[]{:S(2)}, u32[]{:S(2)}) collective-permute-start(bf16[3,64,512]{2,1,0:T(8,128)(2,1)S(1)} %collective-permute-done.7.rest_1_), channel_id=1, source_target_pairs={{0,1},{1,2},{2,3},{3,0},{4,5},{5,6},{6,7},{7,4},{8,9},{9,10},{10,1... | collective-permute-start | bytes 589832 | tf_op jit(solution)/shard_map/ppermute | solution.py:208
  23.9 1.2 collective-permute-done.9.rest_3_
  25.1 3.1 %collective-permute-start.6 = (bf16[3,64,512]{2,1,0:T(8,128)(2,1)S(1)}, bf16[3,64,512]{2,1,0:T(8,128)(2,1)S(1)}, u32[]{:S(2)}, u32[]{:S(2)}) collective-permute-start(bf16[3,64,512]{2,1,0:T(8,128)(2,1)S(1)} %squeeze.31.after.here.rest_0_.before), channel_id=1, source_target_pairs={{0,3},{1,0},{2,1},{3,2},{4,7},{5,4},{6,5},{7,6},{8,11},{9,8},{10,9... | collective-permute-start | bytes 589832 | tf_op jit(solution)/shard_map/ppermute | solution.py:208
  28.2 2.5 %collective-permute-done.4.rest_1_ = bf16[3,64,512]{2,1,0:T(8,128)(2,1)S(1)} collective-permute-done((bf16[3,64,512]{2,1,0:T(8,128)(2,1)S(1)}, bf16[3,64,512]{2,1,0:T(8,128)(2,1)S(1)}, u32[]{:S(2)}, u32[]{:S(2)}) %collective-permute-start.4) | collective-permute-done | bytes 196640 | tf_op jit(solution)/shard_map/ppermute | solution.py:208
  30.8 4.1 %collective-permute-done.1.rest_1_ = bf16[3,64,512]{2,1,0:T(8,128)(2,1)S(1)} collective-permute-done((bf16[3,64,512]{2,1,0:T(8,128)(2,1)S(1)}, bf16[3,64,512]{2,1,0:T(8,128)(2,1)S(1)}, u32[]{:S(2)}, u32[]{:S(2)}) %collective-permute-start.1) | collective-permute-done | bytes 196640 | tf_op jit(solution)/shard_map/ppermute | solution.py:208
  34.9 4.2 %collective-permute-done.12.rest_2_ = bf16[3,64,512]{2,1,0:T(8,128)(2,1)S(1)} collective-permute-done((bf16[3,64,512]{2,1,0:T(8,128)(2,1)S(1)}, bf16[3,64,512]{2,1,0:T(8,128)(2,1)S(1)}, u32[]{:S(2)}, u32[]{:S(2)}) %collective-permute-start.12) | collective-permute-done | bytes 196640 | tf_op jit(solution)/shard_map/ppermute | solution.py:208
  39.1 1.4 %collective-permute-start.3 = (bf16[3,64,512]{2,1,0:T(8,128)(2,1)S(1)}, bf16[3,64,512]{2,1,0:T(8,128)(2,1)S(1)}, u32[]{:S(2)}, u32[]{:S(2)}) collective-permute-start(bf16[3,64,512]{2,1,0:T(8,128)(2,1)S(1)} %squeeze.32.after.here.rest_0_), channel_id=1, source_target_pairs={{0,3},{1,0},{2,1},{3,2},{4,7},{5,4},{6,5},{7,6},{8,11},{9,8},{10,9... | collective-permute-start | bytes 589832 | tf_op jit(solution)/shard_map/ppermute | solution.py:208
  40.5 2.8 %collective-permute-done.8.rest_2_ = bf16[3,64,512]{2,1,0:T(8,128)(2,1)S(1)} collective-permute-done((bf16[3,64,512]{2,1,0:T(8,128)(2,1)S(1)}, bf16[3,64,512]{2,1,0:T(8,128)(2,1)S(1)}, u32[]{:S(2)}, u32[]{:S(2)}) %collective-permute-start.8) | collective-permute-done | bytes 196640 | tf_op jit(solution)/shard_map/ppermute | solution.py:208
  43.3 1.6 %collective-permute-start.2 = (bf16[3,64,512]{2,1,0:T(8,128)(2,1)S(1)}, bf16[3,64,512]{2,1,0:T(8,128)(2,1)S(1)}, u32[]{:S(2)}, u32[]{:S(2)}) collective-permute-start(bf16[3,64,512]{2,1,0:T(8,128)(2,1)S(1)} %collective-permute-done.1.rest_1_), channel_id=1, source_target_pairs={{0,1},{1,2},{2,3},{3,0},{4,5},{5,6},{6,7},{7,4},{8,9},{9,10},{10,1... | collective-permute-start | bytes 589832 | tf_op jit(solution)/shard_map/ppermute | solution.py:208
  45.0 11.9 %plane_terms.4.rest_4_ = f32[256,5632]{1,0:T(8,128)S(1)} custom-call(s32[2]{0:T(128)S(1)} %pad_add_fusion.me_ref, bf16[3,64,512]{2,1,0:T(8,128)(2,1)S(1)} %collective-permute-done.10.before, bf16[3,64,512]{2,1,0:T(8,128)(2,1)S(1)} %squeeze.33.here.rest_0_.before, bf16[3,64,512]{2,1,0:T(8,128)(2,1)S(1)} %squeeze.34.after.here.rest_0_.before, ...), custom_call_target="tpu_custom_call" | custom-call | tf_op jit(solution)/shard_map/plane_terms/pallas_call | solution.py:166
  56.9 12.0 %plane_terms.5.rest_4_ = f32[256,5632]{1,0:T(8,128)S(1)} custom-call(s32[2]{0:T(128)S(1)} %pad_add_fusion.me_ref, bf16[3,64,512]{2,1,0:T(8,128)(2,1)S(1)} %squeeze.33.here.rest_0_.before, bf16[3,64,512]{2,1,0:T(8,128)(2,1)S(1)} %squeeze.34.after.here.rest_0_.before, ...), custom_call_target="tpu_custom_call", output_to_operand_aliasing={{}: (8, {})} | custom-call | tf_op jit(solution)/shard_map/plane_terms/pallas_call | solution.py:166
  68.9 12.0 %plane_terms.6.rest_4_ = f32[256,5632]{1,0:T(8,128)S(1)} custom-call(s32[2]{0:T(128)S(1)} %pad_add_fusion.me_ref, bf16[3,64,512]{2,1,0:T(8,128)(2,1)S(1)} %squeeze.34.after.here.rest_0_.before, bf16[3,64,512]{2,1,0:T(8,128)(2,1)S(1)} %squeeze.31.after.here.rest_0_.before, ...), custom_call_target="tpu_custom_call", output_to_operand_aliasing={{}: (8, {})} | custom-call | tf_op jit(solution)/shard_map/plane_terms/pallas_call | solution.py:166
  83.0 0.9 copy-done.3
  85.8 13.1 %plane_terms.7 = (f32[128,5632]{1,0:T(8,128)S(1)}, bf16[128,5632]{1,0:T(8,128)(2,1)}) custom-call(s32[2]{0:T(128)S(1)} %pad_add_fusion.me_ref, bf16[3,64,512]{2,1,0:T(8,128)(2,1)S(1)} %squeeze.31.after.here.rest_0_.before, bf16[3,64,512]{2,1,0:T(8,128)(2,1)S(1)} %squeeze.32.after.here.rest_0_, bf16[3,64,512]{2,1,0:T(8,128)(2,1)S(1)} %copy-done.3, ...), custom_call_target="tpu_custom_call" | custom-call | tf_op jit(solution)/shard_map/plane_terms/pallas_call | solution.py:166
  98.9 3.6 %collective-permute-done.14 = bf16[128,5632]{1,0:T(8,128)(2,1)} collective-permute-done((bf16[128,5632]{1,0:T(8,128)(2,1)}, bf16[128,5632]{1,0:T(8,128)(2,1)}, u32[]{:S(2)}, u32[]{:S(2)}) %collective-permute-start.14) | collective-permute-done | bytes 1441824 | tf_op jit(solution)/shard_map/ppermute | solution.py:237
  102.4 1.6 %convert_add_fusion = f32[128,5632]{1,0:T(8,128)S(1)} fusion(f32[128,5632]{1,0:T(8,128)S(1)} %get-tuple-element.5, bf16[128,5632]{1,0:T(8,128)(2,1)} %collective-permute-done.14), kind=kLoop, calls=%fused_computation | loop fusion | flops 1441792 | bytes 7208960 | tf_op jit(solution)/shard_map/add | solution.py:237
  104.4 1.6 %collective-permute-start.17 = (bf16[2,32,2816]{2,1,0:T(8,128)(2,1)S(1)}, bf16[2,32,2816]{2,1,0:T(8,128)(2,1)}, u32[]{:S(2)}, u32[]{:S(2)}) collective-permute-start(bf16[2,32,2816]{2,1,0:T(8,128)(2,1)S(1)} %fusion), channel_id=1, source_target_pairs={{0,16},{4,20},{8,24},{12,28},{16,0},{20,4},{24,8},{28,12},{1,17},{... | collective-permute-start | bytes 1081352 | tf_op jit(solution)/shard_map/ppermute | solution.py:197
  106.0 2.6 %collective-permute-start.15 = (bf16[2,32,2816]{2,1,0:T(8,128)(2,1)S(1)}, bf16[2,32,2816]{2,1,0:T(8,128)(2,1)S(1)}, u32[]{:S(2)}, u32[]{:S(2)}) collective-permute-start(bf16[2,32,2816]{2,1,0:T(8,128)(2,1)S(1)} %fusion.1), channel_id=1, source_target_pairs={{0,8},{4,12},{8,0},{12,4},{16,24},{20,28},{24,16},{28,20},{1,9},{5... | collective-permute-start | bytes 1081352 | tf_op jit(solution)/shard_map/ppermute | solution.py:197
  108.6 6.4 %collective-permute-done.17 = bf16[2,32,2816]{2,1,0:T(8,128)(2,1)} collective-permute-done((bf16[2,32,2816]{2,1,0:T(8,128)(2,1)S(1)}, bf16[2,32,2816]{2,1,0:T(8,128)(2,1)}, u32[]{:S(2)}, u32[]{:S(2)}) %collective-permute-start.17) | collective-permute-done | bytes 360480 | tf_op jit(solution)/shard_map/ppermute | solution.py:197
  115.0 1.0 bitcast_add_fusion.1
  116.1 2.4 %collective-permute-start.18 = (bf16[32,2816]{1,0:T(8,128)(2,1)S(1)}, bf16[32,2816]{1,0:T(8,128)(2,1)S(1)}, u32[]{:S(2)}, u32[]{:S(2)}) collective-permute-start(bf16[32,2816]{1,0:T(8,128)(2,1)S(1)} %fusion.5), channel_id=1, source_target_pairs={{0,8},{4,12},{8,0},{12,4},{16,24},{20,28},{24,16},{28,20},{1,9},{5... | collective-permute-start | bytes 540680 | tf_op jit(solution)/shard_map/ppermute | solution.py:197
  118.6 1.8 %collective-permute-start.16 = (bf16[32,2816]{1,0:T(8,128)(2,1)S(1)}, bf16[32,2816]{1,0:T(8,128)(2,1)S(1)}, u32[]{:S(2)}, u32[]{:S(2)}) collective-permute-start(bf16[32,2816]{1,0:T(8,128)(2,1)S(1)} %fusion.4), channel_id=1, source_target_pairs={{0,16},{4,20},{8,24},{12,28},{16,0},{20,4},{24,8},{28,12},{1,17},{... | collective-permute-start | bytes 540680 | tf_op jit(solution)/shard_map/ppermute | solution.py:197
  120.4 2.4 %collective-permute-done.18 = bf16[32,2816]{1,0:T(8,128)(2,1)S(1)} collective-permute-done((bf16[32,2816]{1,0:T(8,128)(2,1)S(1)}, bf16[32,2816]{1,0:T(8,128)(2,1)S(1)}, u32[]{:S(2)}, u32[]{:S(2)}) %collective-permute-start.18) | collective-permute-done | bytes 180256 | tf_op jit(solution)/shard_map/ppermute | solution.py:197
  (52 shorter events, 8.7 us)
Async XLA Ops:
  2.7 10.9 %collective-permute-start.11 = (bf16[3,64,512]{2,1,0:T(8,128)(2,1)S(1)}, bf16[3,64,512]{2,1,0:T(8,128)(2,1)S(1)}, u32[]{:S(2)}, u32[]{:S(2)}) collective-permute-start(bf16[3,64,512]{2,1,0:T(8,128)(2,1)S(1)} %squeeze.33.here.rest_0_.before), channel_id=1, source_target_pairs={{0,1},{1,2},{2,3},{3,0},{4,5},{5,6},{6,7},{7,4},{8,9},{9,10},{10,1... | collective-permute-start | bytes 589832 | tf_op jit(solution)/shard_map/ppermute | solution.py:208
  5.9 12.6 %collective-permute-start.13 = (bf16[3,64,512]{2,1,0:T(8,128)(2,1)S(1)}, bf16[3,64,512]{2,1,0:T(8,128)(2,1)S(1)}, u32[]{:S(2)}, u32[]{:S(2)}) collective-permute-start(bf16[3,64,512]{2,1,0:T(8,128)(2,1)S(1)} %squeeze.33.here.rest_0_.before), channel_id=1, source_target_pairs={{0,3},{1,0},{2,1},{3,2},{4,7},{5,4},{6,5},{7,6},{8,11},{9,8},{10,9... | collective-permute-start | bytes 589832 | tf_op jit(solution)/shard_map/ppermute | solution.py:208
  8.1 7.4 %collective-permute-start.10 = (bf16[3,64,512]{2,1,0:T(8,128)(2,1)S(1)}, bf16[3,64,512]{2,1,0:T(8,128)(2,1)S(1)}, u32[]{:S(2)}, u32[]{:S(2)}) collective-permute-start(bf16[3,64,512]{2,1,0:T(8,128)(2,1)S(1)} %squeeze.32.after.here.rest_0_), channel_id=1, source_target_pairs={{0,4},{4,8},{8,12},{12,16},{16,20},{20,24},{24,28},{28,0},{1,5},{5... | collective-permute-start | bytes 589832 | tf_op jit(solution)/shard_map/ppermute | solution.py:225
  8.3 13.8 %collective-permute-start.7 = (bf16[3,64,512]{2,1,0:T(8,128)(2,1)S(1)}, bf16[3,64,512]{2,1,0:T(8,128)(2,1)S(1)}, u32[]{:S(2)}, u32[]{:S(2)}) collective-permute-start(bf16[3,64,512]{2,1,0:T(8,128)(2,1)S(1)} %squeeze.34.after.here.rest_0_.before), channel_id=1, source_target_pairs={{0,1},{1,2},{2,3},{3,0},{4,5},{5,6},{6,7},{7,4},{8,9},{9,10},{10,1... | collective-permute-start | bytes 589832 | tf_op jit(solution)/shard_map/ppermute | solution.py:208
  8.4 16.7 %collective-permute-start.9 = (bf16[3,64,512]{2,1,0:T(8,128)(2,1)S(1)}, bf16[3,64,512]{2,1,0:T(8,128)(2,1)S(1)}, u32[]{:S(2)}, u32[]{:S(2)}) collective-permute-start(bf16[3,64,512]{2,1,0:T(8,128)(2,1)S(1)} %squeeze.34.after.here.rest_0_.before), channel_id=1, source_target_pairs={{0,3},{1,0},{2,1},{3,2},{4,7},{5,4},{6,5},{7,6},{8,11},{9,8},{10,9... | collective-permute-start | bytes 589832 | tf_op jit(solution)/shard_map/ppermute | solution.py:208
  13.7 17.0 %collective-permute-start.4 = (bf16[3,64,512]{2,1,0:T(8,128)(2,1)S(1)}, bf16[3,64,512]{2,1,0:T(8,128)(2,1)S(1)}, u32[]{:S(2)}, u32[]{:S(2)}) collective-permute-start(bf16[3,64,512]{2,1,0:T(8,128)(2,1)S(1)} %squeeze.31.after.here.rest_0_.before), channel_id=1, source_target_pairs={{0,1},{1,2},{2,3},{3,0},{4,5},{5,6},{6,7},{7,4},{8,9},{9,10},{10,1... | collective-permute-start | bytes 589832 | tf_op jit(solution)/shard_map/ppermute | solution.py:208
  15.5 19.4 %collective-permute-start.1 = (bf16[3,64,512]{2,1,0:T(8,128)(2,1)S(1)}, bf16[3,64,512]{2,1,0:T(8,128)(2,1)S(1)}, u32[]{:S(2)}, u32[]{:S(2)}) collective-permute-start(bf16[3,64,512]{2,1,0:T(8,128)(2,1)S(1)} %squeeze.32.after.here.rest_0_), channel_id=1, source_target_pairs={{0,1},{1,2},{2,3},{3,0},{4,5},{5,6},{6,7},{7,4},{8,9},{9,10},{10,1... | collective-permute-start | bytes 589832 | tf_op jit(solution)/shard_map/ppermute | solution.py:208
  18.5 20.6 %collective-permute-start.12 = (bf16[3,64,512]{2,1,0:T(8,128)(2,1)S(1)}, bf16[3,64,512]{2,1,0:T(8,128)(2,1)S(1)}, u32[]{:S(2)}, u32[]{:S(2)}) collective-permute-start(bf16[3,64,512]{2,1,0:T(8,128)(2,1)S(1)} %collective-permute-done.11.rest_1_), channel_id=1, source_target_pairs={{0,1},{1,2},{2,3},{3,0},{4,5},{5,6},{6,7},{7,4},{8,9},{9,10},{10,1... | collective-permute-start | bytes 589832 | tf_op jit(solution)/shard_map/ppermute | solution.py:208
  22.1 21.1 %collective-permute-start.8 = (bf16[3,64,512]{2,1,0:T(8,128)(2,1)S(1)}, bf16[3,64,512]{2,1,0:T(8,128)(2,1)S(1)}, u32[]{:S(2)}, u32[]{:S(2)}) collective-permute-start(bf16[3,64,512]{2,1,0:T(8,128)(2,1)S(1)} %collective-permute-done.7.rest_1_), channel_id=1, source_target_pairs={{0,1},{1,2},{2,3},{3,0},{4,5},{5,6},{6,7},{7,4},{8,9},{9,10},{10,1... | collective-permute-start | bytes 589832 | tf_op jit(solution)/shard_map/ppermute | solution.py:208
  25.1 43.9 %collective-permute-start.6 = (bf16[3,64,512]{2,1,0:T(8,128)(2,1)S(1)}, bf16[3,64,512]{2,1,0:T(8,128)(2,1)S(1)}, u32[]{:S(2)}, u32[]{:S(2)}) collective-permute-start(bf16[3,64,512]{2,1,0:T(8,128)(2,1)S(1)} %squeeze.31.after.here.rest_0_.before), channel_id=1, source_target_pairs={{0,3},{1,0},{2,1},{3,2},{4,7},{5,4},{6,5},{7,6},{8,11},{9,8},{10,9... | collective-permute-start | bytes 589832 | tf_op jit(solution)/shard_map/ppermute | solution.py:208
  30.7 50.3 %collective-permute-start = (bf16[3,64,512]{2,1,0:T(8,128)(2,1)S(1)}, bf16[3,64,512]{2,1,0:T(8,128)(2,1)S(1)}, u32[]{:S(2)}, u32[]{:S(2)}) collective-permute-start(bf16[3,64,512]{2,1,0:T(8,128)(2,1)S(1)} %squeeze.33.here.rest_0_.before), channel_id=1, source_target_pairs={{0,28},{4,0},{8,4},{12,8},{16,12},{20,16},{24,20},{28,24},{1,29},{... | collective-permute-start | bytes 589832 | tf_op jit(solution)/shard_map/ppermute | solution.py:227
  34.9 22.0 %copy-start = (bf16[3,64,512]{2,1,0:T(8,128)(2,1)}, bf16[3,64,512]{2,1,0:T(8,128)(2,1)S(1)}, u32[]{:S(2)}) copy-start(bf16[3,64,512]{2,1,0:T(8,128)(2,1)S(1)} %collective-permute-done.1.rest_1_) | copy-start | bytes 589828
  34.9 34.0 %collective-permute-start.5 = (bf16[3,64,512]{2,1,0:T(8,128)(2,1)S(1)}, bf16[3,64,512]{2,1,0:T(8,128)(2,1)S(1)}, u32[]{:S(2)}, u32[]{:S(2)}) collective-permute-start(bf16[3,64,512]{2,1,0:T(8,128)(2,1)S(1)} %collective-permute-done.4.rest_1_), channel_id=1, source_target_pairs={{0,1},{1,2},{2,3},{3,0},{4,5},{5,6},{6,7},{7,4},{8,9},{9,10},{10,1... | collective-permute-start | bytes 589832 | tf_op jit(solution)/shard_map/ppermute | solution.py:208
  39.1 42.5 %collective-permute-start.3 = (bf16[3,64,512]{2,1,0:T(8,128)(2,1)S(1)}, bf16[3,64,512]{2,1,0:T(8,128)(2,1)S(1)}, u32[]{:S(2)}, u32[]{:S(2)}) collective-permute-start(bf16[3,64,512]{2,1,0:T(8,128)(2,1)S(1)} %squeeze.32.after.here.rest_0_), channel_id=1, source_target_pairs={{0,3},{1,0},{2,1},{3,2},{4,7},{5,4},{6,5},{7,6},{8,11},{9,8},{10,9... | collective-permute-start | bytes 589832 | tf_op jit(solution)/shard_map/ppermute | solution.py:208
  43.3 39.1 %collective-permute-start.2 = (bf16[3,64,512]{2,1,0:T(8,128)(2,1)S(1)}, bf16[3,64,512]{2,1,0:T(8,128)(2,1)S(1)}, u32[]{:S(2)}, u32[]{:S(2)}) collective-permute-start(bf16[3,64,512]{2,1,0:T(8,128)(2,1)S(1)} %collective-permute-done.1.rest_1_), channel_id=1, source_target_pairs={{0,1},{1,2},{2,3},{3,0},{4,5},{5,6},{6,7},{7,4},{8,9},{9,10},{10,1... | collective-permute-start | bytes 589832 | tf_op jit(solution)/shard_map/ppermute | solution.py:208
  68.9 14.1 %copy-start.1 = (bf16[3,64,512]{2,1,0:T(8,128)(2,1)S(1)}, bf16[3,64,512]{2,1,0:T(8,128)(2,1)}, u32[]{:S(2)}) copy-start(bf16[3,64,512]{2,1,0:T(8,128)(2,1)} %copy-done) | copy-start | bytes 589828
  80.9 0.7 copy-start.2
  81.6 0.7 copy-start.4
  82.3 0.7 copy-start.6
  83.0 0.9 copy-start.3
  83.9 0.9 copy-start.5
  84.8 0.9 copy-start.7
  98.9 3.6 %collective-permute-start.14 = (bf16[128,5632]{1,0:T(8,128)(2,1)}, bf16[128,5632]{1,0:T(8,128)(2,1)}, u32[]{:S(2)}, u32[]{:S(2)}) collective-permute-start(bf16[128,5632]{1,0:T(8,128)(2,1)} %get-tuple-element.6), channel_id=1, source_target_pairs={{0,4},{4,0},{8,12},{12,8},{16,20},{20,16},{24,28},{28,24},{1,5},{5... | collective-permute-start | bytes 4325384 | tf_op jit(solution)/shard_map/ppermute | solution.py:237
  104.4 10.6 %collective-permute-start.17 = (bf16[2,32,2816]{2,1,0:T(8,128)(2,1)S(1)}, bf16[2,32,2816]{2,1,0:T(8,128)(2,1)}, u32[]{:S(2)}, u32[]{:S(2)}) collective-permute-start(bf16[2,32,2816]{2,1,0:T(8,128)(2,1)S(1)} %fusion), channel_id=1, source_target_pairs={{0,16},{4,20},{8,24},{12,28},{16,0},{20,4},{24,8},{28,12},{1,17},{... | collective-permute-start | bytes 1081352 | tf_op jit(solution)/shard_map/ppermute | solution.py:197
  106.0 12.4 %collective-permute-start.15 = (bf16[2,32,2816]{2,1,0:T(8,128)(2,1)S(1)}, bf16[2,32,2816]{2,1,0:T(8,128)(2,1)S(1)}, u32[]{:S(2)}, u32[]{:S(2)}) collective-permute-start(bf16[2,32,2816]{2,1,0:T(8,128)(2,1)S(1)} %fusion.1), channel_id=1, source_target_pairs={{0,8},{4,12},{8,0},{12,4},{16,24},{20,28},{24,16},{28,20},{1,9},{5... | collective-permute-start | bytes 1081352 | tf_op jit(solution)/shard_map/ppermute | solution.py:197
  116.1 6.6 %collective-permute-start.18 = (bf16[32,2816]{1,0:T(8,128)(2,1)S(1)}, bf16[32,2816]{1,0:T(8,128)(2,1)S(1)}, u32[]{:S(2)}, u32[]{:S(2)}) collective-permute-start(bf16[32,2816]{1,0:T(8,128)(2,1)S(1)} %fusion.5), channel_id=1, source_target_pairs={{0,8},{4,12},{8,0},{12,4},{16,24},{20,28},{24,16},{28,20},{1,9},{5... | collective-permute-start | bytes 540680 | tf_op jit(solution)/shard_map/ppermute | solution.py:197
  118.6 5.8 %collective-permute-start.16 = (bf16[32,2816]{1,0:T(8,128)(2,1)S(1)}, bf16[32,2816]{1,0:T(8,128)(2,1)S(1)}, u32[]{:S(2)}, u32[]{:S(2)}) collective-permute-start(bf16[32,2816]{1,0:T(8,128)(2,1)S(1)} %fusion.4), channel_id=1, source_target_pairs={{0,16},{4,20},{8,24},{12,28},{16,0},{20,4},{24,8},{28,12},{1,17},{... | collective-permute-start | bytes 540680 | tf_op jit(solution)/shard_map/ppermute | solution.py:197
